TPU v7x, 32 devices: a whole 2x2x4 slice. The times are simulated.
32 devices in a mesh: dp: 8 (over z, x), head: 4 (over y, core).
Axes of the slice: x: 2, y: 2, z: 4, core: 2. Of those that a mesh axis runs over, the one named last changes fastest.
Arguments:
- residual: bfloat16 [32, 4096], P('dp', 'head'), may hold values from -6 to 6
- query: bfloat16 [32, 32, 128], P('dp', 'head'), may hold values from -4.5 to 4.5
- fresh_token_keys: bfloat16 [32, 8, 128], P('dp', 'head'), may hold values from -4.5 to 4.5
- value_new: bfloat16 [32, 8, 128], P('dp', 'head'), may hold values from -24 to 24
- key_cache: bfloat16 [32, 8, 2048, 128], P('dp', 'head'), may hold values from -6 to 6
- value_cache: bfloat16 [32, 8, 2048, 128], P('dp', 'head'), may hold values from -6 to 6
- lengths: int32 [32], P('dp'), may hold values from 1024 to 2048, as said below
- pages: int32 [32, 8, 64], P('dp', 'head'), may hold values from 0 to 127, as said below
- w_out: bfloat16 [4096, 4096], P('head', 'dp'), may hold values from -0.75 to 0.75
- norm_gain: float32 [4096], P('head'), may hold values from 0.5 to 1.5
- expert_ids: int32 [32, 2], P('dp'), may hold values from 0 to 7, all different within a row; in each aligned block of 4 rows (0 to 3, 4 to 7, ...) at most 2 rows name the same one
- gate_weights: float32 [32, 2], P('dp'), may hold values from 0.1 to 1
- w_in: bfloat16 [8, 2, 4096, 7168], P('dp', None, None, 'head'), may hold values from -0.09375 to 0.09375
- w_down: bfloat16 [8, 7168, 4096], P('dp', 'head'), may hold values from -0.0625 to 0.0625
Outputs:
- layer_out: bfloat16 [32, 4096], P('dp', 'head')
Inputs may be any that keep to these rules, and one draw needn't show every extreme that they name: `lengths`: each request's length; some request has exactly 2048 and some exactly 1024. `pages`: for each request and key head, 64 distinct page numbers, all below ceil(length / 16), always including the page that holds the request's last cached token; in no fixed order. `expert_ids`: per token 2 distinct experts; among the 4 tokens of one dp index no expert is named more than 2 times.
All inputs are finite; a program needn't handle non-finite values.
Results may differ from a plain program's by a relative error of at most 0.012.
Values may be sent and summed in bfloat16 or wider, within the bound.
A program may use at most 128 MiB of HBM per device.

v0:
```python
import jax
import jax.numpy as jnp
from jax import lax
from jax.sharding import PartitionSpec as P

EXPERTS = 8
TOP = 2
PAGE = 16
MOST = 2
EPSILON = 1e-05


def shards(
    residual,
    query,
    fresh_token_keys,
    value_new,
    key_cache,
    value_cache,
    lengths,
    pages,
    w_out,
    norm_gain,
    expert_ids,
    gate_weights,
    w_in,
    w_down,
):
    tok_rows = query.shape[0]
    head_local = query.shape[1]
    head_dim = query.shape[2]
    kv_local = key_cache.shape[1]
    cache_len = key_cache.shape[2]
    page_total = cache_len // PAGE
    group_member_count = head_local // kv_local
    page_numbers = jnp.arange(page_total, dtype=jnp.int32)
    page_chosen = jnp.any(pages[:, :, :, None] == page_numbers[None, None, None, :], axis=2)
    position_chosen = jnp.broadcast_to(
        page_chosen[:, :, :, None], (tok_rows, kv_local, page_total, PAGE)
    ).reshape(tok_rows, kv_local, cache_len)
    position_ids = jnp.arange(cache_len, dtype=jnp.int32)
    in_range = (position_chosen & (position_ids[None, None, :] < lengths[:, None, None]))[
        :, :, None, :
    ]
    grouped_rows = query.reshape(tok_rows, kv_local, group_member_count, head_dim)
    score_scale = head_dim ** (-0.5)
    scores = (
        jnp.einsum("bkgd,bksd->bkgs", grouped_rows, key_cache, preferred_element_type=jnp.float32)
        * score_scale
    )
    own_score = (
        jnp.einsum(
            "luxe,lue->lux", grouped_rows, fresh_token_keys, preferred_element_type=jnp.float32
        )
        * score_scale
    )
    masked = jnp.where(in_range, scores, -1e30)
    row_top = jnp.maximum(jnp.max(masked, axis=-1), own_score)
    expo = jnp.where(in_range, jnp.exp(scores - row_top[..., None]), 0.0)
    own_expo = jnp.exp(own_score - row_top)
    denominator = jnp.sum(expo, axis=-1) + own_expo
    weights = (expo / denominator[..., None]).astype(jnp.bfloat16)
    own_weight = (own_expo / denominator).astype(jnp.bfloat16)
    attended = jnp.einsum(
        "bkgs,bksd->bkgd", weights, value_cache, preferred_element_type=jnp.float32
    )
    attended = (
        attended
        + own_weight.astype(jnp.float32)[..., None] * value_new.astype(jnp.float32)[:, :, None, :]
    )
    attn_rows = attended.reshape(tok_rows, head_local * head_dim).astype(jnp.bfloat16)
    every_row = lax.all_gather(attn_rows, "dp", axis=0, tiled=True)
    column_part = jnp.dot(every_row, w_out, preferred_element_type=jnp.float32)
    head_partial = lax.all_to_all(
        column_part.astype(jnp.bfloat16), "dp", split_axis=0, concat_axis=1, tiled=True
    ).astype(column_part.dtype)
    stream = residual.astype(jnp.float32) + lax.psum_scatter(
        head_partial.astype(jnp.bfloat16), "head", scatter_dimension=1, tiled=True
    ).astype(jnp.float32)
    whole_stream, whole_gain = (
        lax.all_gather(stream, "head", axis=1, tiled=True),
        lax.all_gather(norm_gain, "head", axis=0, tiled=True),
    )
    square_mean_value = jnp.mean(whole_stream * whole_stream, axis=-1)
    normed = (
        whole_stream * lax.rsqrt(square_mean_value + EPSILON)[:, None] * whole_gain[None, :]
    ).astype(jnp.bfloat16)
    group_count = lax.axis_size("dp") // EXPERTS
    assignments = tok_rows * TOP
    flat_ids = expert_ids.reshape(assignments)
    expert_range = jnp.arange(EXPERTS, dtype=jnp.int32)
    onehot = (flat_ids[:, None] == expert_range[None, :]).astype(jnp.int32)
    earlier = jnp.cumsum(onehot, axis=0) - onehot
    slot_index = jnp.sum(earlier * onehot, axis=1)
    target = flat_ids * MOST + slot_index
    placement_map = jnp.arange(EXPERTS * MOST, dtype=jnp.int32)[:, None] == target[None, :]
    token_map = jnp.any(placement_map.reshape(EXPERTS * MOST, tok_rows, TOP), axis=2)
    outgoing = jnp.dot(
        token_map.astype(jnp.bfloat16), normed, preferred_element_type=jnp.float32
    ).astype(jnp.bfloat16)
    width_of_row = outgoing.shape[1]
    outgoing = jnp.broadcast_to(
        outgoing.reshape(EXPERTS, 1, MOST, width_of_row), (EXPERTS, group_count, MOST, width_of_row)
    )
    outgoing = outgoing.reshape(EXPERTS * group_count, MOST, width_of_row)
    arrived = lax.all_to_all(outgoing, "dp", split_axis=0, concat_axis=0, tiled=True)
    senders, slot_count, feature_count = arrived.shape
    flat_rows = arrived.reshape(senders * slot_count, feature_count)
    gate_act = jnp.dot(flat_rows, w_in[0, 0], preferred_element_type=jnp.float32)
    up_act = jnp.dot(flat_rows, w_in[0, 1], preferred_element_type=jnp.float32)
    hidden = (jax.nn.silu(gate_act) * up_act).astype(jnp.bfloat16)
    slab_out = jnp.dot(hidden, w_down[0], preferred_element_type=jnp.float32).reshape(
        senders, slot_count, w_down.shape[2]
    )
    summed_total = lax.psum_scatter(
        slab_out.astype(jnp.bfloat16), "head", scatter_dimension=2, tiled=True
    ).astype(jnp.float32)
    returned = lax.all_to_all(
        summed_total.astype(jnp.bfloat16), "dp", split_axis=0, concat_axis=0, tiled=True
    ).astype(summed_total.dtype)
    local_width = returned.shape[2]
    per_expert = jnp.sum(returned.reshape(EXPERTS, group_count, MOST, local_width), axis=1).reshape(
        EXPERTS * MOST, local_width
    )
    weighted = jnp.where(placement_map, gate_weights.reshape(assignments)[None, :], 0.0)
    combine_map = jnp.sum(weighted.reshape(EXPERTS * MOST, tok_rows, TOP), axis=2)
    mixture = jnp.dot(
        combine_map.T,
        per_expert,
        precision=lax.Precision.HIGHEST,
        preferred_element_type=jnp.float32,
    )
    return (stream + mixture).astype(jnp.bfloat16)


def solution(mesh):
    in_specs = (
        P("dp", "head"),
        P("dp", "head", None),
        P("dp", "head", None),
        P("dp", "head", None),
        P("dp", "head", None, None),
        P("dp", "head", None, None),
        P("dp"),
        P("dp", "head", None),
        P("head", "dp"),
        P("head"),
        P("dp", None),
        P("dp", None),
        P("dp", None, None, "head"),
        P("dp", "head", None),
    )
    out_specs = P("dp", "head")
    return jax.shard_map(shards, mesh=mesh, in_specs=in_specs, out_specs=out_specs, check_vma=False)
```

profile of v0, /device:TPU:0, one launch (start us, length us, event | category | flops | bytes accessed | tf_op | source)
XLA Modules:
  0.0 169.4 jit_solution(6646213300250157299)
XLA Ops:
  6.5 0.0 copy-start
  6.5 0.9 fusion.19
  7.5 0.2 broadcast_in_dim.28
  7.7 0.3 reshape.95
  8.0 0.7 iota_compare_fusion.1
  8.8 0.8 fusion.30
  9.6 3.5 %select_reduce_fusion = (f32[4,2,4]{2,1,0:T(2,128)S(1)}, f32[4,2,4,2048]{3,2,1,0:T(4,128)S(1)}) fusion(pred[4,2,2048]{2,1,0:T(4,128)(4,1)S(1)} %copy.32, bf16[4,2,4,128]{3,2,1,0:T(4,128)(2,1)} %bitcast.52, bf16[4,2,2048,128]{3,2,1,0:T(8,128)(2,1)} %param.18), kind=kOutput, calls=%fused_computation.19 | convolution fusion | flops 16973792 | bytes 4481152 | tf_op jit(solution)/shard_map/bkgd,bksd->bkgs/dot_general | solution.py:48
  13.1 0.3 fusion.20
  13.5 0.7 convert_element_type.55
  14.1 2.9 %fusion.18 = bf16[4,2,4,128]{3,2,1,0:T(4,128)(2,1)S(1)} fusion(bf16[4,2,2048,128]{3,2,1,0:T(8,128)(2,1)} %param.19, f32[4,2,4,2048]{3,2,1,0:T(4,128)S(1)} %get-tuple-element.8, f32[4,2,4]{2,1,0:T(2,128)S(1)} %get-tuple-element.6, f32[4,2,4]{2,1,0:T(2,128)S(1)} %multiply_maximum_fusion, pred[4,2,2048]{2,1,0:T(4,128)(4,1)S(1)} %copy.32, ...), kind=kOutput, calls=%fused_computation.17 | convolution fusion | flops 17051648 | bytes 4485504 | tf_op jit(solution)/shard_map/bkgs,bksd->bkgd/dot_general | solution.py:64
  17.1 32.4 %all-gather = bf16[8,4,1024]{2,1,0:T(4,128)(2,1)S(1)} all-gather(bf16[1,4,1024]{2,1,0:T(4,128)(2,1)S(1)} %reshape.99), channel_id=1, replica_groups=mesh['dp'=8,'head'=4] {'dp'}, dimensions={0}, use_global_device_ids=true | all-gather | bytes 73728 | tf_op jit(solution)/shard_map/all_gather | solution.py:72
  49.5 0.3 convolution_convert_fusion.1
  49.7 0.6 all_to_all.20
  50.4 5.5 %all-to-all-start = ((bf16[8,4,512]{2,1,0:T(4,128)(2,1)}), bf16[8,4,512]{2,1,0:T(4,128)(2,1)S(1)}, u32[]{:S(2)}, u32[]{:S(2)}) async-start(bf16[8,4,512]{2,1,0:T(4,128)(2,1)} %all_to_all.20), calls=%async_computation | async-start | bytes 65536 | tf_op jit(solution)/shard_map/all_to_all | solution.py:74
  55.8 0.0 reduce-scatter.7.cloned.1.call-start
  55.9 0.8 copy.33
  56.7 0.1 eq.47
  56.7 0.1 fusion.28
  56.8 0.2 select_reduce_fusion.2
  57.0 0.1 reduce_sum.44
  57.1 0.1 copy.35
  57.2 5.3 %all_gather.11 = f32[4096]{0:T(1024)S(1)} all-gather(f32[1024]{0:T(1024)} %param.23), channel_id=1, replica_groups=mesh['dp'=8,'head'=4] {'head'}, dimensions={0}, use_global_device_ids=true | all-gather | bytes 20480 | tf_op jit(solution)/shard_map/all_gather | solution.py:82
  62.5 0.0 all-to-all-done
  62.6 1.4 copy.40
  64.0 0.0 reduce-scatter.7.cloned.1.call-update
  64.0 0.0 reduce-scatter.5.cloned.1.call-start
  64.0 0.1 fusion.29
  64.1 26.2 %reduce-scatter.7.cloned.1.call-done = bf16[1024,4]{1,0:T(8,128)(2,1)} async-done(((bf16[4096,4]{1,0:T(8,128)(2,1)}), bf16[1024,4]{1,0:T(8,128)(2,1)}) %reduce-scatter.7.cloned.1.call-update) | async-done | bytes 8208
  90.3 1.1 copy.41
  91.4 0.7 convert_add_fusion
  92.1 5.2 %all_gather.10 = f32[4,4096]{1,0:T(4,128)S(1)} all-gather(f32[4,1024]{1,0:T(4,128)S(1)} %convert_add_fusion), channel_id=1, replica_groups=mesh['dp'=8,'head'=4] {'head'}, dimensions={1}, use_global_device_ids=true | all-gather | bytes 81920 | tf_op jit(solution)/shard_map/all_gather | solution.py:81
  97.3 0.1 multiply_reduce_fusion
  97.5 0.3 convolution_convert_fusion
  97.7 0.1 reshape_reshape.3
  97.8 12.8 %all_to_all.29 = bf16[8,2,4096]{2,1,0:T(2,128)(2,1)S(1)} all-to-all(bf16[8,2,4096]{2,1,0:T(2,128)(2,1)S(1)} %reshape_reshape.3), channel_id=1, replica_groups=mesh['dp'=8,'head'=4] {'dp'}, dimensions={0} | all-to-all | bytes 262144 | tf_op jit(solution)/shard_map/all_to_all | solution.py:106
  110.7 0.1 reshape.97
  110.7 6.2 %fusion.4 = f32[16,1792]{1,0:T(8,128)S(1)} fusion(bf16[16,4096]{1,0:T(8,128)(2,1)S(1)} %reshape.97, bf16[1,2,4096,1792]{3,2,1,0:T(8,128)(2,1)} %param.26), kind=kOutput, calls=%fused_computation.4 | convolution fusion | flops 234881024 | bytes 14925824 | tf_op jit(solution)/shard_map/dot_general | solution.py:109
  117.0 0.0 copy-start.2
  117.0 0.0 copy-start.1
  117.0 6.3 %fusion.14 = bf16[16,1792]{1,0:T(8,128)(2,1)S(1)} fusion(bf16[16,4096]{1,0:T(8,128)(2,1)S(1)} %reshape.97, bf16[1,2,4096,1792]{3,2,1,0:T(8,128)(2,1)} %param.26, f32[16,1792]{1,0:T(8,128)S(1)} %fusion.4), kind=kOutput, calls=%fused_computation.12 | convolution fusion | flops 235053056 | bytes 14983168 | tf_op jit(solution)/shard_map/dot_general | solution.py:110
  123.3 7.8 %fusion.8 = bf16[8,2,4096]{2,0,1:T(8,128)(2,1)} fusion(bf16[1,1792,4096]{2,1,0:T(8,128)(2,1)} %param.27, bf16[8,2,1792]{2,1,0:T(2,128)(2,1)S(1)} %dot_general.36), kind=kOutput, calls=%fused_computation.8 | convolution fusion | flops 234946560 | bytes 14868480 | tf_op jit(solution)/shard_map/dot_general | solution.py:112
  131.1 0.0 reduce-scatter.5.cloned.1.call-update
  131.2 17.0 %reduce-scatter.5.cloned.1.call-done = bf16[8,2,1024]{2,0,1:T(8,128)(2,1)} async-done(((bf16[8,2,4096]{2,0,1:T(8,128)(2,1)}), bf16[8,2,1024]{2,0,1:T(8,128)(2,1)}) %reduce-scatter.5.cloned.1.call-update) | async-done | bytes 32784 | tf_op jit(solution)/shard_map/reduce_scatter | solution.py:115
  148.2 1.4 copy.37
  149.6 5.5 %all-to-all-start.2 = ((bf16[8,2,1024]{2,1,0:T(2,128)(2,1)}), bf16[8,2,1024]{2,1,0:T(2,128)(2,1)S(1)}, u32[]{:S(2)}, u32[]{:S(2)}) async-start(bf16[8,2,1024]{2,1,0:T(2,128)(2,1)} %copy.37), calls=%async_computation.3 | async-start | bytes 65536 | tf_op jit(solution)/shard_map/all_to_all | solution.py:118
  155.1 0.1 select_reduce_fusion.1
  155.2 6.6 %all-to-all-done.2 = bf16[8,2,1024]{2,1,0:T(2,128)(2,1)S(1)} async-done(((bf16[8,2,1024]{2,1,0:T(2,128)(2,1)}), bf16[8,2,1024]{2,1,0:T(2,128)(2,1)S(1)}, u32[]{:S(2)}, u32[]{:S(2)}) %all-to-all-start.2) | async-done | bytes 32800 | tf_op jit(solution)/shard_map/all_to_all | solution.py:118
  161.8 0.7 fusion.17
  (16 shorter events, 0.2 us)
Async XLA Ops:
  6.5 42.9 %copy-start = (bf16[1024,512]{1,0:T(8,128)(2,1)S(1)}, bf16[1024,512]{1,0:T(8,128)(2,1)}, u32[]{:S(2)}) copy-start(bf16[1024,512]{1,0:T(8,128)(2,1)} %param.22) | copy-start | bytes 3145732
  50.4 12.2 %all-to-all-start = ((bf16[8,4,512]{2,1,0:T(4,128)(2,1)}), bf16[8,4,512]{2,1,0:T(4,128)(2,1)S(1)}, u32[]{:S(2)}, u32[]{:S(2)}) async-start(bf16[8,4,512]{2,1,0:T(4,128)(2,1)} %all_to_all.20), calls=%async_computation | async-start | bytes 65536 | tf_op jit(solution)/shard_map/all_to_all | solution.py:74
  55.8 34.5 %reduce-scatter.7.cloned.1.call-start = ((), (), s32[]{:S(2)}) async-start(), calls=%async_computation.6 | async-start | bytes 1310720
  64.0 84.2 %reduce-scatter.5.cloned.1.call-start = ((), (), s32[]{:S(2)}) async-start(), calls=%async_computation.5 | async-start | bytes 163840 | tf_op jit(solution)/shard_map/reduce_scatter | solution.py:115
  117.0 38.1 %copy-start.2 = (f32[4,2]{0,1:T(2,128)S(1)}, f32[4,2]{0,1:T(2,128)}, u32[]{:S(2)}) copy-start(f32[4,2]{0,1:T(2,128)} %param.25) | copy-start | bytes 100
  117.0 44.8 %copy-start.1 = (bf16[4,1024]{1,0:T(4,128)(2,1)S(1)}, bf16[4,1024]{1,0:T(4,128)(2,1)}, u32[]{:S(2)}) copy-start(bf16[4,1024]{1,0:T(4,128)(2,1)} %param.14) | copy-start | bytes 24580
  149.6 12.2 %all-to-all-start.2 = ((bf16[8,2,1024]{2,1,0:T(2,128)(2,1)}), bf16[8,2,1024]{2,1,0:T(2,128)(2,1)S(1)}, u32[]{:S(2)}, u32[]{:S(2)}) async-start(bf16[8,2,1024]{2,1,0:T(2,128)(2,1)} %copy.37), calls=%async_computation.3 | async-start | bytes 65536 | tf_op jit(solution)/shard_map/all_to_all | solution.py:118
Sparse Core Ops, SparseCore 0:
  64.1 26.1 reduce-scatter.6
  131.3 16.8 reduce-scatter.4
where the time goes:
time: 170 us; the launch traced here: 169 us
  blocking collectives  55.7 us (33%)
  waiting for transfers between devices  49.8 us (29%)
  matrix products  28.9 us (17%)
  between operations  13.6 us (8%)
  starting transfers between devices  11.1 us (7%)
  local copies, waits for them, and re-layouts  6.35 us (4%)
  other arithmetic  4 us (2%)
    all_gather x1, blocking collectives, shards(): every_row = lax.all_gather(attn_rows, 'dp', axis=0, tiled=True)  32.4 us
    unnamed x3, waiting for transfers between devices  26.2 us
    reduce_scatter x1, waiting for transfers between devices, shards(): lax.psum_scatter(slab_out.astype(jnp.bfloat16), 'head', scatter_dimension...  17 us
    all_to_all x1, blocking collectives, shards(): lax.all_to_all(outgoing, 'dp', split_axis=0, concat_axis=0, tiled=True)  12.8 us
    dot_general x1, matrix products, shards(): jnp.dot(hidden, w_down[0], preferred_element_type=jnp.float32)  7.82 us
    all_to_all x1, waiting for transfers between devices, shards(): lax.all_to_all(summed_total.astype(jnp.bfloat16), 'dp', split_axis=0, con...  6.6 us
    dot_general x1, matrix products, shards(): up_act = jnp.dot(flat_rows, w_in[0, 1], preferred_element_type=jnp.float32)  6.3 us
    dot_general x1, matrix products, shards(): jnp.dot(flat_rows, w_in[0, 0], preferred_element_type=jnp.float32)  6.24 us
  transfers between devices with their start and end apart: 4, of which 3 were waited for; matrix products, arithmetic and copies ran while one was open for 1% of the time, Pallas kernels for 0%

commit v1 on v0

--- a/solution.py
+++ b/solution.py
@@ -69,7 +69,9 @@
         + own_weight.astype(jnp.float32)[..., None] * value_new.astype(jnp.float32)[:, :, None, :]
     )
     attn_rows = attended.reshape(tok_rows, head_local * head_dim).astype(jnp.bfloat16)
-    every_row = lax.all_gather(attn_rows, "dp", axis=0, tiled=True)
+    every_row = jnp.concatenate(
+        lax.all_to_all(jnp.stack([attn_rows] * lax.axis_size("dp")), "dp", 0, 0), axis=0
+    )
     column_part = jnp.dot(every_row, w_out, preferred_element_type=jnp.float32)
     head_partial = lax.all_to_all(
         column_part.astype(jnp.bfloat16), "dp", split_axis=0, concat_axis=1, tiled=True

time: 170 us -> 149 us (0.88)
  blocking collectives: 55.7 us -> 23.4 us
  waiting for transfers between devices: 49.8 us -> 55.4 us
  starting transfers between devices: 11.1 us -> 16.2 us
    all_gather x1 -> x0, blocking collectives: 32.4 us -> none  [shards(): every_row = lax.all_gather(attn_rows, 'dp', axis=0, tiled=True)]
    all_to_all x0 -> x1, starting transfers between devices: none -> 7.28 us  [shards(): lax.all_to_all(jnp.stack([attn_rows] * lax.axis_size('dp')), 'dp', 0, 0)]
    all_to_all x0 -> x1, waiting for transfers between devices: none -> 5.68 us  [shards(): lax.all_to_all(jnp.stack([attn_rows] * lax.axis_size('dp')), 'dp', 0, 0)]
    all_to_all x1, starting transfers between devices: 5.46 us -> 3.33 us  [shards(): lax.all_to_all(column_part.astype(jnp.bfloat16), 'dp', split_axis=0, conc...]
  transfers between devices with their start and end apart: 4 -> 5, of which waited for: 3 -> 5; matrix products, arithmetic and copies ran while one was open for 1% -> 1% of each run, Pallas kernels for 0% -> 0%
where the time goes in v1:
time: 149 us; the launch traced here: 148 us
  waiting for transfers between devices  55.4 us (37%)
  matrix products  28.9 us (19%)
  blocking collectives  23.4 us (16%)
  starting transfers between devices  16.2 us (11%)
  between operations  13.6 us (9%)
  local copies, waits for them, and re-layouts  6.99 us (5%)
  other arithmetic  4 us (3%)
    unnamed x3, waiting for transfers between devices  25 us
    reduce_scatter x1, waiting for transfers between devices, shards(): lax.psum_scatter(slab_out.astype(jnp.bfloat16), 'head', scatter_dimension...  17 us
    all_to_all x1, blocking collectives, shards(): lax.all_to_all(outgoing, 'dp', split_axis=0, concat_axis=0, tiled=True)  12.8 us
    dot_general x1, matrix products, shards(): jnp.dot(hidden, w_down[0], preferred_element_type=jnp.float32)  7.82 us
    all_to_all x1, starting transfers between devices, shards(): lax.all_to_all(jnp.stack([attn_rows] * lax.axis_size('dp')), 'dp', 0, 0)  7.28 us
    all_to_all x1, waiting for transfers between devices, shards(): lax.all_to_all(summed_total.astype(jnp.bfloat16), 'dp', split_axis=0, con...  6.6 us
    dot_general x1, matrix products, shards(): up_act = jnp.dot(flat_rows, w_in[0, 1], preferred_element_type=jnp.float32)  6.3 us
    dot_general x1, matrix products, shards(): jnp.dot(flat_rows, w_in[0, 0], preferred_element_type=jnp.float32)  6.24 us
  transfers between devices with their start and end apart: 5, of which 5 were waited for; matrix products, arithmetic and copies ran while one was open for 1% of the time, Pallas kernels for 0%

profile of v1, /device:TPU:0, one launch (start us, length us, event | category | flops | bytes accessed | tf_op | source)
XLA Modules:
  0.0 148.4 jit_solution(14691631741744496155)
XLA Ops:
  6.5 0.9 fusion.19
  7.5 0.2 broadcast_in_dim.28
  7.7 0.3 reshape.101
  8.0 0.7 iota_compare_fusion.1
  8.8 0.8 fusion.30
  9.6 3.5 %select_reduce_fusion = (f32[4,2,4]{2,1,0:T(2,128)S(1)}, f32[4,2,4,2048]{3,2,1,0:T(4,128)S(1)}) fusion(pred[4,2,2048]{2,1,0:T(4,128)(4,1)S(1)} %copy.32, bf16[4,2,4,128]{3,2,1,0:T(4,128)(2,1)} %bitcast.52, bf16[4,2,2048,128]{3,2,1,0:T(8,128)(2,1)} %param.18), kind=kOutput, calls=%fused_computation.19 | convolution fusion | flops 16973792 | bytes 4481152 | tf_op jit(solution)/shard_map/bkgd,bksd->bkgs/dot_general | solution.py:48
  13.1 0.3 fusion.20
  13.5 0.7 convert_element_type.57
  14.1 2.9 %fusion.18 = bf16[4,2,4,128]{3,2,1,0:T(4,128)(2,1)S(1)} fusion(bf16[4,2,2048,128]{3,2,1,0:T(8,128)(2,1)} %param.19, f32[4,2,4,2048]{3,2,1,0:T(4,128)S(1)} %get-tuple-element.8, f32[4,2,4]{2,1,0:T(2,128)S(1)} %get-tuple-element.6, f32[4,2,4]{2,1,0:T(2,128)S(1)} %multiply_maximum_fusion, pred[4,2,2048]{2,1,0:T(4,128)(4,1)S(1)} %copy.32, ...), kind=kOutput, calls=%fused_computation.17 | convolution fusion | flops 17051648 | bytes 4485504 | tf_op jit(solution)/shard_map/bkgs,bksd->bkgd/dot_general | solution.py:64
  17.1 0.6 stack.2
  17.7 7.3 %all-to-all-start = ((bf16[8,4,1024]{2,1,0:T(4,128)(2,1)}), bf16[8,4,1024]{2,1,0:T(4,128)(2,1)S(1)}, u32[]{:S(2)}, u32[]{:S(2)}) async-start(bf16[8,4,1024]{2,1,0:T(4,128)(2,1)} %stack.2), calls=%async_computation | async-start | bytes 131072 | tf_op jit(solution)/shard_map/all_to_all | solution.py:73
  25.0 0.8 copy.33
  25.8 0.1 eq.47
  25.9 0.1 fusion.28
  26.0 0.2 select_reduce_fusion.2
  26.2 0.1 reduce_sum.44
  26.2 5.7 %all-to-all-done = bf16[8,4,1024]{2,1,0:T(4,128)(2,1)S(1)} async-done(((bf16[8,4,1024]{2,1,0:T(4,128)(2,1)}), bf16[8,4,1024]{2,1,0:T(4,128)(2,1)S(1)}, u32[]{:S(2)}, u32[]{:S(2)}) %all-to-all-start) | async-done | bytes 65568 | tf_op jit(solution)/shard_map/all_to_all | solution.py:73
  32.0 0.3 convolution_convert_fusion.1
  32.2 0.6 all_to_all.24
  32.9 3.3 %all-to-all-start.1 = ((bf16[8,4,512]{2,1,0:T(4,128)(2,1)}), bf16[8,4,512]{2,1,0:T(4,128)(2,1)S(1)}, u32[]{:S(2)}, u32[]{:S(2)}) async-start(bf16[8,4,512]{2,1,0:T(4,128)(2,1)} %all_to_all.24), calls=%async_computation.1 | async-start | bytes 65536 | tf_op jit(solution)/shard_map/all_to_all | solution.py:76
  36.2 0.0 reduce-scatter.7.cloned.1.call-start
  36.3 0.1 copy.35
  36.4 5.3 %all_gather.7 = f32[4096]{0:T(1024)S(1)} all-gather(f32[1024]{0:T(1024)} %param.23), channel_id=1, replica_groups=mesh['dp'=8,'head'=4] {'head'}, dimensions={0}, use_global_device_ids=true | all-gather | bytes 20480 | tf_op jit(solution)/shard_map/all_gather | solution.py:84
  41.7 1.1 all-to-all-done.1
  42.8 1.4 copy.40
  44.2 0.0 reduce-scatter.7.cloned.1.call-update
  44.3 0.0 reduce-scatter.5.cloned.1.call-start
  44.3 0.1 fusion.29
  44.4 25.0 %reduce-scatter.7.cloned.1.call-done = bf16[1024,4]{1,0:T(8,128)(2,1)} async-done(((bf16[4096,4]{1,0:T(8,128)(2,1)}), bf16[1024,4]{1,0:T(8,128)(2,1)}) %reduce-scatter.7.cloned.1.call-update) | async-done | bytes 8208
  69.4 1.1 copy.41
  70.4 0.7 convert_add_fusion
  71.2 5.2 %all_gather.6 = f32[4,4096]{1,0:T(4,128)S(1)} all-gather(f32[4,1024]{1,0:T(4,128)S(1)} %convert_add_fusion), channel_id=1, replica_groups=mesh['dp'=8,'head'=4] {'head'}, dimensions={1}, use_global_device_ids=true | all-gather | bytes 81920 | tf_op jit(solution)/shard_map/all_gather | solution.py:83
  76.4 0.1 multiply_reduce_fusion
  76.5 0.3 convolution_convert_fusion
  76.8 0.1 reshape_reshape.3
  76.9 12.8 %all_to_all.34 = bf16[8,2,4096]{2,1,0:T(2,128)(2,1)S(1)} all-to-all(bf16[8,2,4096]{2,1,0:T(2,128)(2,1)S(1)} %reshape_reshape.3), channel_id=1, replica_groups=mesh['dp'=8,'head'=4] {'dp'}, dimensions={0} | all-to-all | bytes 262144 | tf_op jit(solution)/shard_map/all_to_all | solution.py:108
  89.7 0.1 reshape.104
  89.8 6.2 %fusion.4 = f32[16,1792]{1,0:T(8,128)S(1)} fusion(bf16[16,4096]{1,0:T(8,128)(2,1)S(1)} %reshape.104, bf16[1,2,4096,1792]{3,2,1,0:T(8,128)(2,1)} %param.26), kind=kOutput, calls=%fused_computation.4 | convolution fusion | flops 234881024 | bytes 14925824 | tf_op jit(solution)/shard_map/dot_general | solution.py:111
  96.0 0.0 copy-start.2
  96.1 6.3 %fusion.14 = bf16[16,1792]{1,0:T(8,128)(2,1)S(1)} fusion(bf16[16,4096]{1,0:T(8,128)(2,1)S(1)} %reshape.104, bf16[1,2,4096,1792]{3,2,1,0:T(8,128)(2,1)} %param.26, f32[16,1792]{1,0:T(8,128)S(1)} %fusion.4), kind=kOutput, calls=%fused_computation.12 | convolution fusion | flops 235053056 | bytes 14983168 | tf_op jit(solution)/shard_map/dot_general | solution.py:112
  102.4 7.8 %fusion.8 = bf16[8,2,4096]{2,0,1:T(8,128)(2,1)} fusion(bf16[1,1792,4096]{2,1,0:T(8,128)(2,1)} %param.27, bf16[8,2,1792]{2,1,0:T(2,128)(2,1)S(1)} %dot_general.36), kind=kOutput, calls=%fused_computation.8 | convolution fusion | flops 234946560 | bytes 14868480 | tf_op jit(solution)/shard_map/dot_general | solution.py:114
  110.2 0.0 reduce-scatter.5.cloned.1.call-update
  110.2 17.0 %reduce-scatter.5.cloned.1.call-done = bf16[8,2,1024]{2,0,1:T(8,128)(2,1)} async-done(((bf16[8,2,4096]{2,0,1:T(8,128)(2,1)}), bf16[8,2,1024]{2,0,1:T(8,128)(2,1)}) %reduce-scatter.5.cloned.1.call-update) | async-done | bytes 32784 | tf_op jit(solution)/shard_map/reduce_scatter | solution.py:117
  127.2 1.4 copy.37
  128.6 5.5 %all-to-all-start.3 = ((bf16[8,2,1024]{2,1,0:T(2,128)(2,1)}), bf16[8,2,1024]{2,1,0:T(2,128)(2,1)S(1)}, u32[]{:S(2)}, u32[]{:S(2)}) async-start(bf16[8,2,1024]{2,1,0:T(2,128)(2,1)} %copy.37), calls=%async_computation.4 | async-start | bytes 65536 | tf_op jit(solution)/shard_map/all_to_all | solution.py:120
  134.2 0.1 select_reduce_fusion.1
  134.2 6.6 %all-to-all-done.3 = bf16[8,2,1024]{2,1,0:T(2,128)(2,1)S(1)} async-done(((bf16[8,2,1024]{2,1,0:T(2,128)(2,1)}), bf16[8,2,1024]{2,1,0:T(2,128)(2,1)S(1)}, u32[]{:S(2)}, u32[]{:S(2)}) %all-to-all-start.3) | async-done | bytes 32800 | tf_op jit(solution)/shard_map/all_to_all | solution.py:120
  140.9 0.7 fusion.17
  (18 shorter events, 0.2 us)
Async XLA Ops:
  6.5 25.4 %copy-start = (bf16[1024,512]{1,0:T(8,128)(2,1)S(1)}, bf16[1024,512]{1,0:T(8,128)(2,1)}, u32[]{:S(2)}) copy-start(bf16[1024,512]{1,0:T(8,128)(2,1)} %param.22) | copy-start | bytes 3145732
  17.7 14.2 %all-to-all-start = ((bf16[8,4,1024]{2,1,0:T(4,128)(2,1)}), bf16[8,4,1024]{2,1,0:T(4,128)(2,1)S(1)}, u32[]{:S(2)}, u32[]{:S(2)}) async-start(bf16[8,4,1024]{2,1,0:T(4,128)(2,1)} %stack.2), calls=%async_computation | async-start | bytes 131072 | tf_op jit(solution)/shard_map/all_to_all | solution.py:73
  32.9 10.0 %all-to-all-start.1 = ((bf16[8,4,512]{2,1,0:T(4,128)(2,1)}), bf16[8,4,512]{2,1,0:T(4,128)(2,1)S(1)}, u32[]{:S(2)}, u32[]{:S(2)}) async-start(bf16[8,4,512]{2,1,0:T(4,128)(2,1)} %all_to_all.24), calls=%async_computation.1 | async-start | bytes 65536 | tf_op jit(solution)/shard_map/all_to_all | solution.py:76
  36.2 33.2 %reduce-scatter.7.cloned.1.call-start = ((), (), s32[]{:S(2)}) async-start(), calls=%async_computation.7 | async-start | bytes 1310720
  44.3 83.0 %reduce-scatter.5.cloned.1.call-start = ((), (), s32[]{:S(2)}) async-start(), calls=%async_computation.6 | async-start | bytes 163840 | tf_op jit(solution)/shard_map/reduce_scatter | solution.py:117
  96.0 38.1 %copy-start.2 = (f32[4,2]{0,1:T(2,128)S(1)}, f32[4,2]{0,1:T(2,128)}, u32[]{:S(2)}) copy-start(f32[4,2]{0,1:T(2,128)} %param.25) | copy-start | bytes 100
  96.0 44.8 %copy-start.1 = (bf16[4,1024]{1,0:T(4,128)(2,1)S(1)}, bf16[4,1024]{1,0:T(4,128)(2,1)}, u32[]{:S(2)}) copy-start(bf16[4,1024]{1,0:T(4,128)(2,1)} %param.14) | copy-start | bytes 24580
  128.6 12.2 %all-to-all-start.3 = ((bf16[8,2,1024]{2,1,0:T(2,128)(2,1)}), bf16[8,2,1024]{2,1,0:T(2,128)(2,1)S(1)}, u32[]{:S(2)}, u32[]{:S(2)}) async-start(bf16[8,2,1024]{2,1,0:T(2,128)(2,1)} %copy.37), calls=%async_computation.4 | async-start | bytes 65536 | tf_op jit(solution)/shard_map/all_to_all | solution.py:120
Sparse Core Ops, SparseCore 0:
  44.4 24.9 reduce-scatter.6
  110.4 16.8 reduce-scatter.4
